TPU v7x, 32 devices: a whole 2x2x4 slice. The times are simulated.
32 devices in a mesh: abl: 2 (over y), head: 4 (over x, core), ctx: 4 (over z).
Axes of the slice: x: 2, y: 2, z: 4, core: 2. Of those that a mesh axis runs over, the one named last changes fastest.
Arguments:
- queries: bfloat16 [1024, 6144], P(('abl', 'head', 'ctx')), parts along dimension 0, may hold values from -30 to 30
- keys: bfloat16 [16384, 6144], P(('abl', 'ctx'), 'head'), parts along dimension 0, may hold values from -6 to 6
- values: bfloat16 [16384, 6144], P(('abl', 'ctx'), 'head'), parts along dimension 0, may hold values from -6 to 6
- kept_rows: int32 [128], P(('abl', 'ctx')), parts along dimension 0, may hold values from 0 to 1, as said below
- out_weight: bfloat16 [6144, 6144], P('head'), may hold values from -6 to 6
Outputs:
- projected: bfloat16 [1024, 6144], P(('abl', 'head', 'ctx')), parts along dimension 0
There are 2 independent parts, one for each index of `abl`. A program takes and returns all parts, laid end to end along the dimension named above; an argument that names none is the same for every part. Nothing has to cross between parts.
Inputs may be any that keep to these rules, and one draw needn't show every extreme that they name: `kept_rows`: in every part the first row of each block of 16 consecutive rows is kept.
All inputs are finite; a program needn't handle non-finite values.
Results may differ from a plain program's by a relative error of at most 0.028.
Values may be sent and summed in bfloat16 or wider, within the bound.
No kernel may reach another device: no remote copies, remote signals or barrier semaphores. Data moves between devices by JAX's collectives and lax.ppermute only.
A program may use at most 128 MiB of HBM per device.

v0:
```python
import math
import jax
import jax.numpy as jnp
from jax import lax
from jax.sharding import PartitionSpec as P

HD = 128


def shards(queries, keys, values, kept_rows, out_weight):
    score_scale = 1.0 / math.sqrt(HD)
    local_heads = keys.shape[1] // HD
    key_count = keys.shape[0]
    key_heads = keys.reshape(key_count, local_heads, HD)
    value_heads = values.reshape(key_count, local_heads, HD)
    visible = jnp.repeat(kept_rows, 128) > 0
    query_block = lax.all_to_all(queries, "head", split_axis=1, concat_axis=0, tiled=True)
    all_queries = lax.all_gather(query_block, "ctx", axis=0, tiled=True)
    row_count = all_queries.shape[0]
    zeros_sum = jnp.zeros((row_count, local_heads * HD), jnp.float32)
    lowest = jnp.full((local_heads, row_count), -1e30, jnp.float32)
    summed = zeros_sum
    row_count = all_queries.shape[0]
    shaped = all_queries.reshape(row_count, local_heads, HD)
    scores = (
        jnp.einsum("qhd,khd->hqk", shaped, key_heads, preferred_element_type=jnp.float32)
        * score_scale
    )
    scores = jnp.where(visible[None, None, :], scores, -jnp.inf)
    highest = jnp.maximum(lowest, jnp.max(scores, axis=-1))
    rescale = jnp.exp(lowest - highest)
    softened = jnp.exp(scores - highest[..., None])
    normal_sum = jnp.sum(softened, axis=-1)
    mixed = jnp.einsum(
        "hqk,khd->qhd",
        softened.astype(jnp.bfloat16),
        value_heads,
        preferred_element_type=jnp.float32,
    )
    summed = summed * jnp.repeat(rescale.T, HD, axis=1) + mixed.reshape(row_count, local_heads * HD)
    summed, running, normal_sum = (summed, highest, normal_sum)
    highest = lax.pmax(running, "ctx")
    rescale = jnp.exp(running - highest)
    summed = summed * jnp.repeat(rescale.T, HD, axis=1)
    normal_sum = normal_sum * rescale
    summed, normal_sum = (
        lax.psum_scatter(
            summed.astype(jnp.bfloat16), "ctx", scatter_dimension=0, tiled=True
        ).astype(jnp.float32),
        lax.psum_scatter(
            normal_sum.astype(jnp.bfloat16), "ctx", scatter_dimension=1, tiled=True
        ).astype(jnp.float32),
    )
    attended = (summed / jnp.repeat(normal_sum.T, HD, axis=1)).astype(jnp.bfloat16)
    return lax.psum_scatter(
        jnp.dot(attended, out_weight, preferred_element_type=jnp.float32).astype(jnp.bfloat16),
        "head",
        scatter_dimension=0,
        tiled=True,
    )


def solution(mesh):
    placed = (
        P(("abl", "head", "ctx"), None),
        P(("abl", "ctx"), "head"),
        P(("abl", "ctx"), "head"),
        P(("abl", "ctx")),
        P("head", None),
    )
    return jax.shard_map(
        shards,
        mesh=mesh,
        in_specs=placed,
        out_specs=P(("abl", "head", "ctx"), None),
        check_vma=False,
    )
```

profile of v0, /device:TPU:0, one launch (start us, length us, event | category | flops | bytes accessed | tf_op | source)
XLA Modules:
  0.0 223.1 jit_solution(14071060724346164999)
XLA Ops:
  6.5 0.0 copy-start
  6.5 0.0 all-gather.2.cloned.1.call-start
  6.5 1.0 copy.33
  7.6 11.6 %all_to_all.19 = bf16[32,4,1536]{2,0,1:T(8,128)(2,1)} all-to-all(bf16[32,4,1536]{2,0,1:T(8,128)(2,1)S(1)} %bitcast.42), channel_id=1, replica_groups=mesh['abl'=2,'head'=4,'ctx'=4] {'head'}, dimensions={1} | all-to-all | bytes 786432 | tf_op jit(solution)/shard_map/all_to_all | solution.py:17
  19.1 0.0 all-gather.2.cloned.1.call-update
  19.2 0.0 reduce-scatter.12.cloned.1.call-start
  19.2 8.8 %copy.21 = bf16[2048,1536]{0,1:T(8,128)(2,1)} copy(bf16[2048,1536]{1,0:T(8,128)(2,1)} %param.6) | data formatting | bytes 12582912 | tf_op args[1]
  28.0 8.8 %copy.24 = bf16[2048,1536]{0,1:T(8,128)(2,1)} copy(bf16[2048,1536]{1,0:T(8,128)(2,1)} %param.7) | data formatting | bytes 12582912 | tf_op args[2]
  36.7 0.0 copy-done
  36.7 0.1 broadcast_bitcast_fusion
  36.8 20.3 %all-gather.2.cloned.1.call-done = bf16[512,1536]{1,0:T(8,128)(2,1)} async-done(((bf16[128,1536]{1,0:T(8,128)(2,1)}), bf16[512,1536]{1,0:T(8,128)(2,1)}) %all-gather.2.cloned.1.call-update) | async-done | bytes 1572880 | tf_op jit(solution)/shard_map/all_gather | solution.py:18
  57.1 1.7 copy.20
  58.8 22.6 %fusion = (f32[12,512]{1,0:T(8,128)S(1)}, f32[12,512,2048]{2,1,0:T(8,128)}) fusion(pred[2048]{0:T(1024)(128)(4,1)S(1)} %broadcast_bitcast_fusion, bf16[512,12,128]{0,2,1:T(8,128)(2,1)S(1)} %bitcast.38, bf16[2048,12,128]{0,2,1:T(8,128)(2,1)} %bitcast.37), kind=kOutput, calls=%fused_computation.2 | convolution fusion | flops 3258968064 | bytes 58222592 | tf_op jit(solution)/shard_map/qhd,khd->hqk/dot_general | solution.py:26
  81.4 16.9 %pmax.7 = f32[12,512]{1,0:T(8,128)S(1)} all-reduce(f32[12,512]{1,0:T(8,128)S(1)} %broadcast_maximum_fusion), channel_id=1, replica_groups=mesh['abl'=2,'head'=4,'ctx'=4] {'ctx'}, use_global_device_ids=true, to_apply=%region_1.2 | all-reduce | flops 6144 | bytes 49152 | tf_op jit(solution)/shard_map/pmax | solution.py:42
  98.4 21.1 %fusion.1 = f32[12,512]{1,0:T(8,128)S(1)} fusion(f32[12,512,2048]{2,1,0:T(8,128)} %get-tuple-element.9, f32[12,512]{1,0:T(8,128)S(1)} %broadcast_maximum_fusion, pred[2048]{0:T(1024)(128)(4,1)S(1)} %broadcast_bitcast_fusion), kind=kLoop, calls=%fused_computation.3 | loop fusion | flops 50325504 | bytes 50382848 | tf_op jit(solution)/shard_map/reduce_sum | solution.py:33
  119.5 0.8 copy.29
  120.3 0.0 reduce-scatter.12.cloned.1.call-update
  120.3 0.0 reduce-scatter.10.cloned.1.call-start
  120.4 22.0 %fusion.7 = bf16[512,12,128]{0,2,1:T(8,128)(2,1)S(1)} fusion(bf16[2048,12,128]{0,2,1:T(8,128)(2,1)} %bitcast.39, f32[12,512,2048]{2,1,0:T(8,128)} %get-tuple-element.9, f32[12,512]{1,0:T(8,128)S(1)} %broadcast_maximum_fusion, pred[2048]{0:T(1024)(128)(4,1)S(1)} %broadcast_bitcast_fusion, f32[512,12]{0,1:T(8,128)S(1)} %get-tuple-element.6, ...), kind=kOutput, calls=%fused_computation.10 | convolution fusion | flops 3273916416 | bytes 58271744 | tf_op jit(solution)/shard_map/hqk,khd->qhd/dot_general | solution.py:34
  142.4 1.6 copy.27
  144.0 0.0 reduce-scatter.10.cloned.1.call-update
  144.0 0.2 reduce-scatter.8.cloned.1.call-start
  144.2 0.0 reduce-scatter.12.cloned.1.call-done
  144.3 0.8 copy.30
  145.1 32.7 %reduce-scatter.10.cloned.1.call-done = bf16[128,1536]{1,0:T(8,128)(2,1)} async-done(((bf16[512,1536]{1,0:T(8,128)(2,1)}), bf16[128,1536]{1,0:T(8,128)(2,1)}) %reduce-scatter.10.cloned.1.call-update) | async-done | bytes 393232
  177.7 1.2 copy.28
  179.0 0.1 fusion.10
  179.1 10.2 %convolution_convert_fusion = bf16[128,6144]{1,0:T(8,128)(2,1)} fusion(bf16[128,1536]{0,1:T(8,128)(2,1)S(1)} %fusion.10, bf16[1536,6144]{1,0:T(8,128)(2,1)} %param.9), kind=kOutput, calls=%fused_computation.7 | convolution fusion | flops 2416705536 | bytes 20840448 | tf_op jit(solution)/shard_map/dot_general | solution.py:56
  189.3 0.0 reduce-scatter.8.cloned.1.call-update
  189.3 27.3 %reduce-scatter.8.cloned.1.call-done = bf16[32,6144]{1,0:T(8,128)(2,1)} async-done(((bf16[128,6144]{1,0:T(8,128)(2,1)}), bf16[32,6144]{1,0:T(8,128)(2,1)}) %reduce-scatter.8.cloned.1.call-update) | async-done | bytes 393232 | tf_op jit(solution)/shard_map/reduce_scatter | solution.py:55
  (4 shorter events, 0.0 us)
Async XLA Ops:
  6.5 30.2 %copy-start = (s32[16]{0:T(128)S(1)}, s32[16]{0:T(128)}, u32[]{:S(2)}) copy-start(s32[16]{0:T(128)} %param.8) | copy-start | bytes 196
  6.5 50.6 %all-gather.2.cloned.1.call-start = ((), (), s32[]{:S(2)}) async-start(), calls=%async_computation.4 | async-start | bytes 1966080 | tf_op jit(solution)/shard_map/all_gather | solution.py:18
  19.2 125.1 %reduce-scatter.12.cloned.1.call-start = ((), (), s32[]{:S(2)}) async-start(), calls=%async_computation.7 | async-start | bytes 163840
  120.3 57.4 %reduce-scatter.10.cloned.1.call-start = ((), (), s32[]{:S(2)}) async-start(), calls=%async_computation.6 | async-start | bytes 1966080
  144.0 72.6 %reduce-scatter.8.cloned.1.call-start = ((), (), s32[]{:S(2)}) async-start(), calls=%async_computation.5 | async-start | bytes 1966080 | tf_op jit(solution)/shard_map/reduce_scatter | solution.py:55
Sparse Core Ops, SparseCore 0:
  19.3 37.8 all-gather.1
  120.4 17.4 reduce-scatter.11
  144.1 33.5 reduce-scatter.9
  189.4 27.1 reduce-scatter.7
where the time goes:
time: 224 us; the launch traced here: 223 us
  waiting for transfers between devices  80.4 us (36%)
  matrix products  54.9 us (25%)
  blocking collectives  28.5 us (13%)
  local copies, waits for them, and re-layouts  24.7 us (11%)
  other arithmetic  21.2 us (9%)
  between operations  13.2 us (6%)
    unnamed x6, waiting for transfers between devices  32.7 us
    reduce_scatter x1, waiting for transfers between devices, shards(): lax.psum_scatter(jnp.dot(attended, out_weight, preferred_element_type=jnp...  27.3 us
    dot_general x1, matrix products, shards(): jnp.einsum('qhd,khd->hqk', shaped, key_heads, preferred_element_type=jnp....  22.6 us
    dot_general x1, matrix products, shards(): jnp.einsum('hqk,khd->qhd', softened.astype(jnp.bfloat16), value_heads, pr...  22 us
    unnamed x8, local copies, waits for them, and re-layouts  21.9 us
    reduce_sum x1, other arithmetic, shards(): normal_sum = jnp.sum(softened, axis=-1)  21.1 us
    all_gather x1, waiting for transfers between devices, shards(): all_queries = lax.all_gather(query_block, 'ctx', axis=0, tiled=True)  20.3 us
    pmax x1, blocking collectives, shards(): highest = lax.pmax(running, 'ctx')  16.9 us
  transfers between devices with their start and end apart: 4, of which 3 were waited for; matrix products, arithmetic and copies ran while one was open for 19% of the time, Pallas kernels for 0%

commit v1 on v0

--- a/solution.py
+++ b/solution.py
@@ -5,6 +5,12 @@
 from jax.sharding import PartitionSpec as P
 
 HD = 128
+
+
+def in_order(blocks, dim):
+    shape = list(blocks.shape[1:])
+    shape[dim] *= blocks.shape[0]
+    return jnp.moveaxis(blocks, 0, dim).reshape(shape)
 
 
 def shards(queries, keys, values, kept_rows, out_weight):
@@ -15,7 +21,19 @@
     value_heads = values.reshape(key_count, local_heads, HD)
     visible = jnp.repeat(kept_rows, 128) > 0
     query_block = lax.all_to_all(queries, "head", split_axis=1, concat_axis=0, tiled=True)
-    all_queries = lax.all_gather(query_block, "ctx", axis=0, tiled=True)
+    size = lax.axis_size("ctx")
+    pairs = [(i, (i + 1) % size) for i in range(size)]
+    back = [(b, a) for a, b in pairs]
+    lower, upper = ([], [])
+    for step in range(size - 1):
+        if step % 2 == 0:
+            lower.append(lax.ppermute(lower[-1] if lower else query_block, "ctx", pairs))
+        else:
+            upper.append(lax.ppermute(upper[-1] if upper else query_block, "ctx", back))
+    parts = jnp.stack([*lower[::-1], query_block, *upper])
+    shift = lax.axis_index("ctx") - len(lower)
+    parts = parts[(jnp.arange(size) - shift) % size]
+    all_queries = in_order(parts, 0)
     row_count = all_queries.shape[0]
     zeros_sum = jnp.zeros((row_count, local_heads * HD), jnp.float32)
     lowest = jnp.full((local_heads, row_count), -1e30, jnp.float32)

time: 224 us -> 229 us (1.022)
  starting transfers between devices: 0.31 us -> 4.15 us
  local copies, waits for them, and re-layouts: 24.7 us -> 27.6 us
  waiting for transfers between devices: 80.4 us -> 77.6 us
    all_gather x1 -> x0, waiting for transfers between devices: 20.3 us -> none  [shards(): all_queries = lax.all_gather(query_block, 'ctx', axis=0, tiled=True)]
    ppermute x0 -> x3, waiting for transfers between devices: none -> 18.3 us  [the longest x1 9.47 us: shards(): upper.append(lax.ppermute(upper[-1] if upper else query_block, 'ctx', back))]
    ppermute x0 -> x3, starting transfers between devices: none -> 3.88 us  [the longest x1 2.3 us: shards(): upper.append(lax.ppermute(upper[-1] if upper else query_block, 'ctx', back))]
    another operation x0 -> x1, local copies, waits for them, and re-layouts: none -> 2.89 us  [shards(): shaped = all_queries.reshape(row_count, local_heads, HD)]
    unnamed x6 -> x5, waiting for transfers between devices: 32.7 us -> 32 us
  transfers between devices with their start and end apart: 4 -> 6, of which waited for: 3 -> 4; matrix products, arithmetic and copies ran while one was open for 19% -> 18% of each run, Pallas kernels for 0% -> 0%
where the time goes in v1:
time: 229 us; the launch traced here: 228 us
  waiting for transfers between devices  77.6 us (34%)
  matrix products  55.2 us (24%)
  blocking collectives  28.9 us (13%)
  local copies, waits for them, and re-layouts  27.6 us (12%)
  other arithmetic  21.4 us (9%)
  between operations  13.2 us (6%)
  starting transfers between devices  4.15 us (2%)
    unnamed x5, waiting for transfers between devices  32 us
    reduce_scatter x1, waiting for transfers between devices, shards(): lax.psum_scatter(jnp.dot(attended, out_weight, preferred_element_type=jnp...  27.3 us
    dot_general x1, matrix products, shards(): jnp.einsum('qhd,khd->hqk', shaped, key_heads, preferred_element_type=jnp....  22.9 us
    dot_general x1, matrix products, shards(): jnp.einsum('hqk,khd->qhd', softened.astype(jnp.bfloat16), value_heads, pr...  22 us
    unnamed x8, local copies, waits for them, and re-layouts  21.8 us
    reduce_sum x1, other arithmetic, shards(): normal_sum = jnp.sum(softened, axis=-1)  21.1 us
    pmax x1, blocking collectives, shards(): highest = lax.pmax(running, 'ctx')  17.4 us
    all_to_all x1, blocking collectives, shards(): lax.all_to_all(queries, 'head', split_axis=1, concat_axis=0, tiled=True)  11.5 us
  transfers between devices with their start and end apart: 6, of which 4 were waited for; matrix products, arithmetic and copies ran while one was open for 18% of the time, Pallas kernels for 0%

profile of v1, /device:TPU:0, one launch (start us, length us, event | category | flops | bytes accessed | tf_op | source)
XLA Modules:
  0.0 228.0 jit_solution(7476263701949374718)
XLA Ops:
  6.5 0.0 reduce-scatter.12.cloned.1.call-start
  6.5 1.0 copy.41
  7.6 11.5 %all_to_all.19 = bf16[32,4,1536]{2,0,1:T(8,128)(2,1)S(1)} all-to-all(bf16[32,4,1536]{2,0,1:T(8,128)(2,1)S(1)} %bitcast.48), channel_id=1, replica_groups=mesh['abl'=2,'head'=4,'ctx'=4] {'head'}, dimensions={1} | all-to-all | bytes 786432 | tf_op jit(solution)/shard_map/all_to_all | solution.py:23
  19.0 1.6 collective-permute-start
  20.6 8.7 %copy.22 = bf16[2048,1536]{0,1:T(8,128)(2,1)} copy(bf16[2048,1536]{1,0:T(8,128)(2,1)} %param.6) | data formatting | bytes 12582912 | tf_op args[1]
  29.3 0.0 copy-start
  29.3 8.7 %copy.25 = bf16[2048,1536]{0,1:T(8,128)(2,1)} copy(bf16[2048,1536]{1,0:T(8,128)(2,1)} %param.7) | data formatting | bytes 12582912 | tf_op args[2]
  38.0 2.3 %collective-permute-start.2 = (bf16[128,1536]{1,0:T(8,128)(2,1)S(1)}, bf16[128,1536]{1,0:T(8,128)(2,1)S(1)}, u32[]{:S(2)}, u32[]{:S(2)}) collective-permute-start(bf16[128,1536]{1,0:T(8,128)(2,1)S(1)} %bitcast.46), channel_id=1, source_target_pairs={{1,0},{2,1},{3,2},{0,3},{5,4},{6,5},{7,6},{4,7},{9,8},{10,9},{11,1... | collective-permute-start | bytes 1179656 | tf_op jit(solution)/shard_map/ppermute | solution.py:32
  40.3 0.0 collective-permute-done
  40.3 0.0 collective-permute-start.1
  40.3 0.0 copy-done
  40.4 0.1 broadcast_bitcast_fusion
  40.4 9.5 %collective-permute-done.2 = bf16[128,1536]{1,0:T(8,128)(2,1)S(1)} collective-permute-done((bf16[128,1536]{1,0:T(8,128)(2,1)S(1)}, bf16[128,1536]{1,0:T(8,128)(2,1)S(1)}, u32[]{:S(2)}, u32[]{:S(2)}) %collective-permute-start.2) | collective-permute-done | bytes 393248 | tf_op jit(solution)/shard_map/ppermute | solution.py:32
  49.9 8.8 %collective-permute-done.1 = bf16[128,1536]{1,0:T(8,128)(2,1)S(1)} collective-permute-done((bf16[128,1536]{1,0:T(8,128)(2,1)S(1)}, bf16[128,1536]{1,0:T(8,128)(2,1)S(1)}, u32[]{:S(2)}, u32[]{:S(2)}) %collective-permute-start.1) | collective-permute-done | bytes 393248 | tf_op jit(solution)/shard_map/ppermute | solution.py:30
  58.7 0.2 pad_maximum_fusion
  58.9 1.8 gather_fusion
  60.7 2.9 %reshape.94 = bf16[512,12,128]{2,1,0:T(8,128)(2,1)S(1)} reshape(bf16[4,128,1536]{2,1,0:T(8,128)(2,1)} %gather_fusion) | data formatting | bytes 3145728 | tf_op jit(solution)/shard_map/reshape;reshape | solution.py:42
  63.6 22.9 %fusion = (f32[12,512]{1,0:T(8,128)S(1)}, f32[12,512,2048]{2,1,0:T(8,128)}) fusion(pred[2048]{0:T(1024)(128)(4,1)S(1)} %broadcast_bitcast_fusion, bf16[2048,12,128]{0,2,1:T(8,128)(2,1)} %bitcast.42, bf16[512,12,128]{2,1,0:T(8,128)(2,1)S(1)} %reshape.94), kind=kOutput, calls=%fused_computation.3 | convolution fusion | flops 3258968064 | bytes 58222592 | tf_op jit(solution)/shard_map/qhd,khd->hqk/dot_general | solution.py:44
  86.6 17.4 %pmax.7 = f32[12,512]{1,0:T(8,128)S(1)} all-reduce(f32[12,512]{1,0:T(8,128)S(1)} %broadcast_maximum_fusion), channel_id=1, replica_groups=mesh['abl'=2,'head'=4,'ctx'=4] {'ctx'}, use_global_device_ids=true, to_apply=%region_1.2 | all-reduce | flops 6144 | bytes 49152 | tf_op jit(solution)/shard_map/pmax | solution.py:60
  104.0 21.1 %fusion.1 = f32[12,512]{1,0:T(8,128)S(1)} fusion(f32[12,512,2048]{2,1,0:T(8,128)} %get-tuple-element.9, f32[12,512]{1,0:T(8,128)S(1)} %broadcast_maximum_fusion, pred[2048]{0:T(1024)(128)(4,1)S(1)} %broadcast_bitcast_fusion), kind=kLoop, calls=%fused_computation.4 | loop fusion | flops 50325504 | bytes 50382848 | tf_op jit(solution)/shard_map/reduce_sum | solution.py:51
  125.1 0.8 copy.33
  125.9 0.0 reduce-scatter.12.cloned.1.call-update
  125.9 0.0 reduce-scatter.10.cloned.1.call-start
  126.0 22.0 %fusion.7 = bf16[512,12,128]{0,2,1:T(8,128)(2,1)S(1)} fusion(bf16[2048,12,128]{0,2,1:T(8,128)(2,1)} %bitcast.43, f32[12,512,2048]{2,1,0:T(8,128)} %get-tuple-element.9, f32[12,512]{1,0:T(8,128)S(1)} %broadcast_maximum_fusion, pred[2048]{0:T(1024)(128)(4,1)S(1)} %broadcast_bitcast_fusion, f32[512,12]{0,1:T(8,128)S(1)} %get-tuple-element.6, ...), kind=kOutput, calls=%fused_computation.11 | convolution fusion | flops 3273916416 | bytes 58271744 | tf_op jit(solution)/shard_map/hqk,khd->qhd/dot_general | solution.py:52
  148.0 1.6 copy.31
  149.6 0.0 reduce-scatter.10.cloned.1.call-update
  149.6 0.2 reduce-scatter.8.cloned.1.call-start
  149.9 0.0 reduce-scatter.12.cloned.1.call-done
  149.9 0.8 copy.34
  150.7 31.9 %reduce-scatter.10.cloned.1.call-done = bf16[128,1536]{1,0:T(8,128)(2,1)} async-done(((bf16[512,1536]{1,0:T(8,128)(2,1)}), bf16[128,1536]{1,0:T(8,128)(2,1)}) %reduce-scatter.10.cloned.1.call-update) | async-done | bytes 393232
  182.6 1.2 copy.32
  183.8 0.1 fusion.12
  183.9 10.2 %convolution_convert_fusion = bf16[128,6144]{1,0:T(8,128)(2,1)} fusion(bf16[128,1536]{0,1:T(8,128)(2,1)S(1)} %fusion.12, bf16[1536,6144]{1,0:T(8,128)(2,1)} %param.9), kind=kOutput, calls=%fused_computation.8 | convolution fusion | flops 2416705536 | bytes 20840448 | tf_op jit(solution)/shard_map/dot_general | solution.py:74
  194.2 0.0 reduce-scatter.8.cloned.1.call-update
  194.2 27.3 %reduce-scatter.8.cloned.1.call-done = bf16[32,6144]{1,0:T(8,128)(2,1)} async-done(((bf16[128,6144]{1,0:T(8,128)(2,1)}), bf16[32,6144]{1,0:T(8,128)(2,1)}) %reduce-scatter.8.cloned.1.call-update) | async-done | bytes 393232 | tf_op jit(solution)/shard_map/reduce_scatter | solution.py:73
  (6 shorter events, 0.1 us)
Async XLA Ops:
  6.5 143.4 %reduce-scatter.12.cloned.1.call-start = ((), (), s32[]{:S(2)}) async-start(), calls=%async_computation.6 | async-start | bytes 163840
  19.0 21.3 %collective-permute-start = (bf16[128,1536]{1,0:T(8,128)(2,1)S(1)}, bf16[128,1536]{1,0:T(8,128)(2,1)S(1)}, u32[]{:S(2)}, u32[]{:S(2)}) collective-permute-start(bf16[128,1536]{1,0:T(8,128)(2,1)S(1)} %bitcast.45), channel_id=1, source_target_pairs={{0,1},{1,2},{2,3},{3,0},{4,5},{5,6},{6,7},{7,4},{8,9},{9,10},{10,1... | collective-permute-start | bytes 1179656 | tf_op jit(solution)/shard_map/ppermute | solution.py:30
  29.3 11.0 %copy-start = (s32[16]{0:T(128)S(1)}, s32[16]{0:T(128)}, u32[]{:S(2)}) copy-start(s32[16]{0:T(128)} %param.8) | copy-start | bytes 196
  38.0 11.9 %collective-permute-start.2 = (bf16[128,1536]{1,0:T(8,128)(2,1)S(1)}, bf16[128,1536]{1,0:T(8,128)(2,1)S(1)}, u32[]{:S(2)}, u32[]{:S(2)}) collective-permute-start(bf16[128,1536]{1,0:T(8,128)(2,1)S(1)} %bitcast.46), channel_id=1, source_target_pairs={{1,0},{2,1},{3,2},{0,3},{5,4},{6,5},{7,6},{4,7},{9,8},{10,9},{11,1... | collective-permute-start | bytes 1179656 | tf_op jit(solution)/shard_map/ppermute | solution.py:32
  40.3 18.4 %collective-permute-start.1 = (bf16[128,1536]{1,0:T(8,128)(2,1)S(1)}, bf16[128,1536]{1,0:T(8,128)(2,1)S(1)}, u32[]{:S(2)}, u32[]{:S(2)}) collective-permute-start(bf16[128,1536]{1,0:T(8,128)(2,1)S(1)} %collective-permute-done), channel_id=1, source_target_pairs={{0,1},{1,2},{2,3},{3,0},{4,5},{5,6},{6,7},{7,4},{8,9},{9,10},{10,1... | collective-permute-start | bytes 1179656 | tf_op jit(solution)/shard_map/ppermute | solution.py:30
  125.9 56.7 %reduce-scatter.10.cloned.1.call-start = ((), (), s32[]{:S(2)}) async-start(), calls=%async_computation.5 | async-start | bytes 1966080
  149.6 71.9 %reduce-scatter.8.cloned.1.call-start = ((), (), s32[]{:S(2)}) async-start(), calls=%async_computation.4 | async-start | bytes 1966080 | tf_op jit(solution)/shard_map/reduce_scatter | solution.py:73
Sparse Core Ops, SparseCore 0:
  126.1 16.7 reduce-scatter.11
  149.8 32.8 reduce-scatter.9
  194.3 27.1 reduce-scatter.7
